TPU v7x, 32 devices: a whole 2x2x4 slice. The times are simulated.
32 devices in a mesh: fx: 2 (over y), fy: 4 (over x, core), st: 4 (over z).
Axes of the slice: x: 2, y: 2, z: 4, core: 2. Of those that a mesh axis runs over, the one named last changes fastest.
Arguments:
- tangent_rhs: bfloat16 [4, 6, 64, 2, 4, 128], P('st', None, None, 'fx', 'fy'), may hold values from -6 to 6
- adjoint_rhs: bfloat16 [4, 6, 64, 2, 4, 128], P('st', None, None, 'fx', 'fy'), may hold values from -6 to 6
- jacobians: bfloat16 [3, 6, 6, 2, 4, 128], P(None, None, None, 'fx', 'fy'), may hold values from -0.75 to 0.75
- deriv: bfloat16 [3, 64, 64], replicated, may hold values from -0.75 to 0.75
- penalty: float32 [6], replicated, may hold values from 0.1 to 0.4
- second_order: float32 [6, 2, 4, 128], P(None, 'fx', 'fy'), may hold values from -4 to 4
- coupling: bfloat16 [6, 384], replicated, may hold values from -2.5 to 2.5
- shell_inverse: bfloat16 [16, 384, 384], P('st')
- shell_load: float32 [4, 16, 384], P(None, 'st'), may hold values from -6 to 6
- shell_adjoint_rhs: float32 [4, 16, 384], P(None, 'st'), may hold values from -6 to 6
- iface_elem: int32 [8, 128], P(('fx', 'fy')), may hold values from 0 to 127
- iface_node: int32 [8, 128], P(('fx', 'fy')), may hold values from 0 to 1023
- iface_weight: float32 [8, 128], P(('fx', 'fy')), may hold values from 0.5 to 2
- iface_count: int32 [8], P(('fx', 'fy')), may hold values from 0 to 128, as said below
Outputs:
- tangent_flow: bfloat16 [4, 6, 64, 2, 4, 128], P('st', None, None, 'fx', 'fy')
- adjoint_flow: bfloat16 [4, 6, 64, 2, 4, 128], P('st', None, None, 'fx', 'fy')
- shell_tangent: float32 [4, 16, 384], P(None, 'st')
- shell_adjoint: float32 [4, 16, 384], P(None, 'st')
Inputs may be any that keep to these rules, and one draw needn't show every extreme that they name: `iface_count`: at most 128 live slots in one flow block; some block has exactly 128.
All inputs are finite; a program needn't handle non-finite values.
Results may differ from a plain program's by a relative error of at most 0.0069.
Values may be sent and summed in bfloat16 or wider, within the bound.
No kernel may reach another device: no remote copies, remote signals or barrier semaphores. Data moves between devices by JAX's collectives and lax.ppermute only.
A program may use at most 64 MiB of HBM per device.

v0:
```python
import jax
import jax.numpy as jnp
from jax import lax
from jax.sharding import PartitionSpec as P

SDOF = 6
PN = 64
FSWEEP = 3
ROUNDS = 2
SIGMA = 0.5


def with_halo(value, sides, width):
    for axis, dim in sides:
        peers, length = (lax.axis_size(axis), value.shape[dim])
        up = [(i, (i + 1) % peers) for i in range(peers - 1)]
        down = [(j, i) for i, j in up]
        last = lax.slice_in_dim(value, length - width, length, axis=dim)
        initial = lax.slice_in_dim(value, 0, width, axis=dim)
        before = lax.ppermute(last, axis, up)
        after = lax.ppermute(initial, axis, down)
        value = jnp.concatenate([before, value, after], axis=dim)
    return value


def face_pair(lower_face, upper_face, below, above, axis):
    length = lower_face.shape[axis]
    beyond_upper = jnp.concatenate(
        [lax.slice_in_dim(lower_face, 1, length, axis=axis), above], axis=axis
    )
    beyond_lower = jnp.concatenate(
        [below, lax.slice_in_dim(upper_face, 0, length - 1, axis=axis)], axis=axis
    )
    return (lower_face - beyond_lower, upper_face - beyond_upper)


def place_faces(jump_low, jump_high, axis):
    middle_shape = list(jump_low.shape)
    middle_shape.insert(axis, 2)
    middle = jnp.zeros(middle_shape, jump_low.dtype)
    return jnp.concatenate(
        [jnp.expand_dims(jump_low, axis), middle, jnp.expand_dims(jump_high, axis)], axis=axis
    )


def as_cube(values):
    members, variables, points, size_x, size_y, size_z = values.shape
    return values.reshape(members, variables, 4, 4, 4, size_x, size_y, size_z)


def face_edges(values):
    cube = as_cube(values)
    received = []
    for node_axis in (2, 3):
        elem_axis = node_axis + 2
        lower_face = jnp.take(cube, 0, axis=node_axis)
        upper_face = jnp.take(cube, 3, axis=node_axis)
        edges = jnp.concatenate([lower_face, upper_face], axis=elem_axis)
        if node_axis == 2:
            extended = with_halo(edges, (("fx", 4),), 1)
        else:
            extended = with_halo(edges, (("fy", 5),), 1)
        below = lax.slice_in_dim(extended, 0, 1, axis=elem_axis)
        above = lax.slice_in_dim(extended, 3, 4, axis=elem_axis)
        received.append((below, above))
    return received


def flow_jumps(values, received):
    cube = as_cube(values)
    result = jnp.zeros(cube.shape, jnp.float32)
    for node_axis in (2, 3, 4):
        elem_axis = node_axis + 2
        lower_face = jnp.take(cube, 0, axis=node_axis).astype(jnp.float32)
        upper_face = jnp.take(cube, 3, axis=node_axis).astype(jnp.float32)
        if received is None or node_axis == 4:
            below = jnp.zeros_like(lax.slice_in_dim(lower_face, 0, 1, axis=elem_axis))
            above = below
        else:
            below = received[node_axis - 2][0].astype(jnp.float32)
            above = received[node_axis - 2][1].astype(jnp.float32)
        jump_low, jump_high = face_pair(lower_face, upper_face, below, above, elem_axis)
        result = result + place_faces(jump_low, jump_high, node_axis)
    return result.reshape(values.shape)


def volume(values, deriv_mats, jac_mats):
    grads = jnp.einsum("kpq,vqxyz->kvpxyz", deriv_mats, values, preferred_element_type=jnp.float32)
    result = jnp.sum(jac_mats[0][:, :, None] * grads[0][None], axis=1)
    for axis_index in (1, 2):
        result = result + jnp.sum(
            jac_mats[axis_index][:, :, None] * grads[axis_index][None], axis=1
        )
    return result


def operator(states, operator_kinds, penalty):
    values = lax.optimization_barrier(states.astype(jnp.bfloat16))
    received = face_edges(values)
    jumps = flow_jumps(values, received)
    volumes = jnp.stack(
        [
            volume(values[member], operator_kinds[member][0], operator_kinds[member][1])
            for member in range(len(operator_kinds))
        ]
    )
    return states + volumes + penalty[None, :, None, None, None, None] * jumps


def body(
    tangent_rhs,
    adjoint_rhs,
    jacobians,
    deriv,
    penalty,
    second_order,
    coupling,
    shell_inverse,
    shell_load,
    shell_adjoint_rhs,
    iface_elem,
    iface_node,
    iface_weight,
    iface_count,
):
    state_shape = tangent_rhs.shape
    variables = state_shape[1]
    points = state_shape[2]
    elements = state_shape[3] * state_shape[4] * state_shape[5]
    slots = iface_elem.shape[1]
    live = (jnp.arange(slots, dtype=jnp.int32) < iface_count[0]).astype(jnp.float32)
    weights = iface_weight[0] * live
    elem_index = iface_elem[0]
    node_index = iface_node[0]
    dof_rows = jnp.arange(SDOF, dtype=jnp.int32)[:, None]
    columns = (node_index // PN)[None, :] * (SDOF * PN) + dof_rows * PN + (node_index % PN)[None, :]
    forward_jac = jacobians.astype(jnp.float32)
    forward_kind = (deriv, forward_jac)
    backward_kind = (jnp.swapaxes(deriv, 1, 2), jnp.swapaxes(forward_jac, 1, 2))
    coupling_cols = coupling.T

    def shell_solve(rhs):
        return jnp.einsum(
            "pab,dpb->dpa",
            shell_inverse,
            rhs.astype(jnp.bfloat16),
            preferred_element_type=jnp.float32,
        )

    shell_tangent = shell_solve(shell_load)
    shell_adjoint = jnp.zeros(shell_load.shape, jnp.float32)
    tangent = jnp.zeros(state_shape, jnp.float32)
    adjoint = jnp.zeros(state_shape, jnp.float32)
    for round_index in range(ROUNDS):
        received = lax.all_to_all(
            shell_tangent.astype(jnp.bfloat16), "st", split_axis=0, concat_axis=1, tiled=True
        )
        picked = received.reshape(-1)[columns]
        pushed_cols = (
            jnp.dot(coupling_cols, picked, preferred_element_type=jnp.float32) * weights[None, :]
        )
        pushed = (
            jnp.zeros((variables * points, elements), jnp.float32)
            .at[:, elem_index]
            .add(pushed_cols)
        )
        force = tangent_rhs.astype(jnp.float32) - pushed.reshape(state_shape)
        adjoint_source = adjoint_rhs.astype(jnp.float32) + second_order[None, :, None] * tangent
        paired = jnp.concatenate([tangent, adjoint])
        sources = jnp.concatenate([force, adjoint_source])
        for sweep in range(FSWEEP):
            paired = paired + SIGMA * (
                sources - operator(paired, (forward_kind, backward_kind), penalty)
            )
        tangent = paired[:1]
        adjoint = paired[1:]
        adjoint_values = adjoint.astype(jnp.bfloat16).reshape(variables * points, elements)
        gathered = adjoint_values[:, elem_index]
        loads = jnp.dot(coupling, gathered, preferred_element_type=jnp.float32) * weights[None, :]
        panels = received.shape[1]
        partial_loads = jnp.zeros((panels * SDOF * PN,), jnp.float32).at[columns].add(loads)
        partial_loads = partial_loads.reshape(1, panels, SDOF * PN)
        summed = lax.psum(partial_loads, ("fx", "fy"))
        owned = lax.all_to_all(summed, "st", split_axis=1, concat_axis=0, tiled=True)
        shell_adjoint = shell_solve(shell_adjoint_rhs - owned)
        shell_tangent = shell_solve(shell_load + shell_adjoint)
    return (
        tangent.astype(jnp.bfloat16),
        adjoint.astype(jnp.bfloat16),
        shell_tangent,
        shell_adjoint,
    )


def solution(mesh):
    in_specs = (
        P("st", None, None, "fx", "fy", None),
        P("st", None, None, "fx", "fy", None),
        P(None, None, None, "fx", "fy", None),
        P(),
        P(),
        P(None, "fx", "fy", None),
        P(),
        P("st", None, None),
        P(None, "st", None),
        P(None, "st", None),
        P(("fx", "fy"), None),
        P(("fx", "fy"), None),
        P(("fx", "fy"), None),
        P(("fx", "fy")),
    )
    out_specs = (
        P("st", None, None, "fx", "fy", None),
        P("st", None, None, "fx", "fy", None),
        P(None, "st", None),
        P(None, "st", None),
    )
    return jax.shard_map(body, mesh=mesh, in_specs=in_specs, out_specs=out_specs, check_vma=False)
```

profile of v0, /device:TPU:0, one launch (start us, length us, event | category | flops | bytes accessed | tf_op | source)
XLA Modules:
  0.0 207.5 jit_solution(6584082621477791752)
XLA Ops:
  0.7 5.0 %collective-permute-start = (bf16[2,6,4,4,1,1,128]{6,3,2,1,0,5,4:T(4,128)(2,1)S(1)}, bf16[2,6,4,4,1,1,128]{6,3,2,1,0,5,4:T(4,128)(2,1)S(1)}, u32[]{:S(2)}, u32[]{:S(2)}) collective-permute-start(bf16[2,6,4,4,1,1,128]{6,3,2,1,0,5,4:T(4,128)(2,1)S(1)} %get-tuple-element.197), channel_id=1, source_target_pairs={{0,16},{1,17},{2,18},{3,19},{4,20},{5,21},{6,22},{7,23},{8,24},{9,... | collective-permute-start | bytes 147464 | tf_op jit(solution)/shard_map/ppermute | solution.py:20
  5.8 1.3 collective-permute-start.1
  7.1 1.5 collective-permute-start.2
  8.6 1.3 collective-permute-start.3
  9.9 0.7 convert_element_type.279
  11.1 0.6 copy.260
  11.7 4.9 %all-to-all-start = ((bf16[4,4,384]{2,1,0:T(4,128)(2,1)}), bf16[4,4,384]{2,1,0:T(4,128)(2,1)S(1)}, u32[]{:S(2)}, u32[]{:S(2)}) async-start(bf16[4,4,384]{2,1,0:T(4,128)(2,1)} %copy.260), calls=%async_computation | async-start | bytes 24576 | tf_op jit(solution)/shard_map/all_to_all | solution.py:155
  21.0 1.2 all-to-all-done
  22.2 5.0 %gather_fusion = bf16[768]{0:T(1024)(128)(2,1)S(1)} fusion(bf16[6144]{0:T(1024)(128)(2,1)S(1)} %reshape.2599, s32[1024]{0:T(1024)S(1)} %pad_clamp_fusion.1), kind=kCustom, calls=%fused_computation | custom fusion | bytes 6144 | tf_op jit(solution)/shard_map/gather | solution.py:158
  27.5 1.4 scatter_custom_fusion
  31.5 4.4 %collective-permute-start.4 = (bf16[2,6,4,4,1,1,128]{6,3,2,1,0,5,4:T(4,128)(2,1)S(1)}, bf16[2,6,4,4,1,1,128]{6,3,2,1,0,5,4:T(4,128)(2,1)S(1)}, u32[]{:S(2)}, u32[]{:S(2)}) collective-permute-start(bf16[2,6,4,4,1,1,128]{6,3,2,1,0,5,4:T(4,128)(2,1)S(1)} %get-tuple-element.187), channel_id=1, source_target_pairs={{0,16},{1,17},{2,18},{3,19},{4,20},{5,21},{6,22},{7,23},{8,24},{9,... | collective-permute-start | bytes 147464 | tf_op jit(solution)/shard_map/ppermute | solution.py:20
  35.9 1.3 collective-permute-start.5
  37.2 3.0 %collective-permute-start.6 = (bf16[2,6,4,4,1,1,128]{6,3,2,1,0,5,4:T(4,128)(2,1)S(1)}, bf16[2,6,4,4,1,1,128]{6,3,2,1,0,5,4:T(4,128)(2,1)S(1)}, u32[]{:S(2)}, u32[]{:S(2)}) collective-permute-start(bf16[2,6,4,4,1,1,128]{6,3,2,1,0,5,4:T(4,128)(2,1)S(1)} %get-tuple-element.185), channel_id=1, source_target_pairs={{0,4},{4,8},{8,12},{1,5},{5,9},{9,13},{2,6},{6,10},{10,14},{3,7},{... | collective-permute-start | bytes 147464 | tf_op jit(solution)/shard_map/ppermute | solution.py:20
  40.3 1.3 collective-permute-start.7
  42.3 4.1 %collective-permute-done.7 = bf16[2,6,4,4,1,1,128]{6,3,2,1,0,5,4:T(4,128)(2,1)S(1)} collective-permute-done((bf16[2,6,4,4,1,1,128]{6,3,2,1,0,5,4:T(4,128)(2,1)S(1)}, bf16[2,6,4,4,1,1,128]{6,3,2,1,0,5,4:T(4,128)(2,1)S(1)}, u32[]{:S(2)}, u32[]{:S(2)}) %collective-permute-start.7) | collective-permute-done | bytes 49184 | tf_op jit(solution)/shard_map/ppermute | solution.py:21
  48.7 4.7 %collective-permute-start.10 = (bf16[2,6,4,4,1,1,128]{6,3,2,1,0,5,4:T(4,128)(2,1)S(1)}, bf16[2,6,4,4,1,1,128]{6,3,2,1,0,5,4:T(4,128)(2,1)S(1)}, u32[]{:S(2)}, u32[]{:S(2)}) collective-permute-start(bf16[2,6,4,4,1,1,128]{6,3,2,1,0,5,4:T(4,128)(2,1)S(1)} %get-tuple-element.175), channel_id=1, source_target_pairs={{0,4},{4,8},{8,12},{1,5},{5,9},{9,13},{2,6},{6,10},{10,14},{3,7},{... | collective-permute-start | bytes 147464 | tf_op jit(solution)/shard_map/ppermute | solution.py:20
  53.4 1.3 collective-permute-start.11
  54.7 4.5 %collective-permute-start.8 = (bf16[2,6,4,4,1,1,128]{6,3,2,1,0,5,4:T(4,128)(2,1)S(1)}, bf16[2,6,4,4,1,1,128]{6,3,2,1,0,5,4:T(4,128)(2,1)S(1)}, u32[]{:S(2)}, u32[]{:S(2)}) collective-permute-start(bf16[2,6,4,4,1,1,128]{6,3,2,1,0,5,4:T(4,128)(2,1)S(1)} %get-tuple-element.177), channel_id=1, source_target_pairs={{0,16},{1,17},{2,18},{3,19},{4,20},{5,21},{6,22},{7,23},{8,24},{9,... | collective-permute-start | bytes 147464 | tf_op jit(solution)/shard_map/ppermute | solution.py:20
  59.3 1.3 collective-permute-start.9
  61.2 4.4 %collective-permute-done.9 = bf16[2,6,4,4,1,1,128]{6,3,2,1,0,5,4:T(4,128)(2,1)S(1)} collective-permute-done((bf16[2,6,4,4,1,1,128]{6,3,2,1,0,5,4:T(4,128)(2,1)S(1)}, bf16[2,6,4,4,1,1,128]{6,3,2,1,0,5,4:T(4,128)(2,1)S(1)}, u32[]{:S(2)}, u32[]{:S(2)}) %collective-permute-start.9) | collective-permute-done | bytes 49184 | tf_op jit(solution)/shard_map/ppermute | solution.py:21
  66.9 0.7 slice_bitcast_fusion.71
  67.6 0.7 slice_bitcast_fusion.69
  68.6 0.8 multiply_reduce_fusion.12
  69.5 0.8 multiply_reduce_fusion.14
  70.4 0.8 slice.579
  71.2 2.1 collective-permute-start.12
  73.4 1.1 gather_fusion.1
  74.5 0.8 fusion.5
  75.3 4.8 %scatter_custom_fusion.1 = f32[6144]{0:T(1024)S(1)} fusion(s32[768]{0:T(1024)} %copy-done.12, f32[768]{0:T(1024)S(1)} %fusion.5, f32[]{:T(128)} %constant.129.clone.1), kind=kCustom, calls=%fused_computation.296 | custom fusion | flops 768 | bytes 25088 | tf_op jit(solution)/shard_map/scatter-add | solution.py:181
  80.0 23.1 %psum.14 = f32[1,16,384]{2,0,1:T(1,128)} all-reduce(f32[1,16,384]{2,0,1:T(1,128)S(1)} %bitcast.739), channel_id=1, replica_groups=mesh['fx'=2,'fy'=4,'st'=4] {'fx','fy'}, use_global_device_ids=true, to_apply=%region_20.27 | all-reduce | flops 6144 | bytes 49152 | tf_op jit(solution)/shard_map/psum | solution.py:183
  103.2 3.9 %all-to-all-start.1 = ((f32[1,16,384]{2,0,1:T(1,128)}), f32[1,16,384]{2,0,1:T(1,128)}, u32[]{:S(2)}, u32[]{:S(2)}) async-start(f32[1,16,384]{2,0,1:T(1,128)} %psum.14), calls=%async_computation.1 | async-start | bytes 49152 | tf_op jit(solution)/shard_map/all_to_all | solution.py:184
  107.1 0.9 convert_add_fusion
  108.1 1.0 add_bitcast_fusion.4
  109.0 0.9 pad_subtract_fusion.4
  110.0 1.3 collective-permute-start.13
  111.3 1.3 collective-permute-start.14
  112.6 1.3 collective-permute-start.15
  113.9 0.8 reduce.36
  114.7 0.7 subtract_convert_fusion.1
  115.4 1.5 fusion.3
  116.9 0.6 copy.301
  117.6 5.1 %all-to-all-start.2 = ((bf16[4,4,384]{2,1,0:T(4,128)(2,1)}), bf16[4,4,384]{2,1,0:T(4,128)(2,1)S(1)}, u32[]{:S(2)}, u32[]{:S(2)}) async-start(bf16[4,4,384]{2,1,0:T(4,128)(2,1)} %copy.301), calls=%async_computation.2 | async-start | bytes 24576 | tf_op jit(solution)/shard_map/all_to_all | solution.py:155
  122.7 0.9 subtract_bitcast_fusion.9
  123.9 4.4 %all-to-all-done.2 = bf16[4,4,384]{2,1,0:T(4,128)(2,1)S(1)} async-done(((bf16[4,4,384]{2,1,0:T(4,128)(2,1)}), bf16[4,4,384]{2,1,0:T(4,128)(2,1)S(1)}, u32[]{:S(2)}, u32[]{:S(2)}) %all-to-all-start.2) | async-done | bytes 12320 | tf_op jit(solution)/shard_map/all_to_all | solution.py:155
  128.3 5.0 %gather_fusion.2 = bf16[768]{0:T(1024)(128)(2,1)S(1)} fusion(bf16[6144]{0:T(1024)(128)(2,1)S(1)} %reshape.2612, s32[1024]{0:T(1024)S(1)} %pad_clamp_fusion.1), kind=kCustom, calls=%fused_computation.2 | custom fusion | bytes 6144 | tf_op jit(solution)/shard_map/gather | solution.py:158
  133.6 1.5 scatter_custom_fusion.2
  137.1 4.5 %collective-permute-start.16 = (bf16[2,6,4,4,1,1,128]{6,3,2,1,0,5,4:T(4,128)(2,1)S(1)}, bf16[2,6,4,4,1,1,128]{6,3,2,1,0,5,4:T(4,128)(2,1)S(1)}, u32[]{:S(2)}, u32[]{:S(2)}) collective-permute-start(bf16[2,6,4,4,1,1,128]{6,3,2,1,0,5,4:T(4,128)(2,1)S(1)} %get-tuple-element.157), channel_id=1, source_target_pairs={{0,16},{1,17},{2,18},{3,19},{4,20},{5,21},{6,22},{7,23},{8,24},{9,... | collective-permute-start | bytes 147464 | tf_op jit(solution)/shard_map/ppermute | solution.py:20
  141.7 1.3 collective-permute-start.17
  143.0 1.3 collective-permute-start.18
  144.3 1.3 collective-permute-start.19
  145.7 1.9 collective-permute-done.17
  147.6 1.9 collective-permute-done.19
  151.2 4.5 %collective-permute-start.20 = (bf16[2,6,4,4,1,1,128]{6,3,2,1,0,5,4:T(4,128)(2,1)S(1)}, bf16[2,6,4,4,1,1,128]{6,3,2,1,0,5,4:T(4,128)(2,1)S(1)}, u32[]{:S(2)}, u32[]{:S(2)}) collective-permute-start(bf16[2,6,4,4,1,1,128]{6,3,2,1,0,5,4:T(4,128)(2,1)S(1)} %get-tuple-element.147), channel_id=1, source_target_pairs={{0,16},{1,17},{2,18},{3,19},{4,20},{5,21},{6,22},{7,23},{8,24},{9,... | collective-permute-start | bytes 147464 | tf_op jit(solution)/shard_map/ppermute | solution.py:20
  155.7 1.3 collective-permute-start.21
  157.0 4.4 %collective-permute-start.22 = (bf16[2,6,4,4,1,1,128]{6,3,2,1,0,5,4:T(4,128)(2,1)S(1)}, bf16[2,6,4,4,1,1,128]{6,3,2,1,0,5,4:T(4,128)(2,1)S(1)}, u32[]{:S(2)}, u32[]{:S(2)}) collective-permute-start(bf16[2,6,4,4,1,1,128]{6,3,2,1,0,5,4:T(4,128)(2,1)S(1)} %get-tuple-element.145), channel_id=1, source_target_pairs={{0,4},{4,8},{8,12},{1,5},{5,9},{9,13},{2,6},{6,10},{10,14},{3,7},{... | collective-permute-start | bytes 147464 | tf_op jit(solution)/shard_map/ppermute | solution.py:20
  161.4 1.3 collective-permute-start.23
  163.6 1.0 collective-permute-done.23
  165.2 0.7 fusion.87
  166.0 1.1 gather_fusion.3
  167.3 4.8 %scatter_custom_fusion.3 = f32[6144]{0:T(1024)S(1)} fusion(s32[768]{0:T(1024)} %copy-done.12, f32[768]{0:T(1024)S(1)} %fusion.4, f32[]{:T(128)} %constant.129.clone.1), kind=kCustom, calls=%fused_computation.294 | custom fusion | flops 768 | bytes 25088 | tf_op jit(solution)/shard_map/scatter-add | solution.py:181
  172.0 25.3 %psum.15 = f32[1,16,384]{2,0,1:T(1,128)S(1)} all-reduce(f32[1,16,384]{2,0,1:T(1,128)S(1)} %bitcast.738), channel_id=1, replica_groups=mesh['fx'=2,'fy'=4,'st'=4] {'fx','fy'}, use_global_device_ids=true, to_apply=%region_41.48 | all-reduce | flops 6144 | bytes 49152 | tf_op jit(solution)/shard_map/psum | solution.py:183
  197.3 8.0 %all_to_all.42 = f32[1,16,384]{2,0,1:T(1,128)S(1)} all-to-all(f32[1,16,384]{2,0,1:T(1,128)S(1)} %psum.15), channel_id=1, replica_groups=mesh['fx'=2,'fy'=4,'st'=4] {'st'}, dimensions={1} | all-to-all | bytes 49152 | tf_op jit(solution)/shard_map/all_to_all | solution.py:184
  206.3 0.6 copy.339
  206.9 0.6 copy.338
  (224 shorter events, 18.9 us)
Async XLA Ops:
  0.6 10.0 %copy-start = (bf16[4,384,384]{2,1,0:T(8,128)(2,1)S(1)}, bf16[4,384,384]{2,1,0:T(8,128)(2,1)}, u32[]{:S(2)}) copy-start(bf16[4,384,384]{2,1,0:T(8,128)(2,1)} %param.33) | copy-start | bytes 3538948
  0.6 16.1 %copy-start.1 = (bf16[3,64,64]{2,1,0:T(8,128)(2,1)S(1)}, bf16[3,64,64]{2,1,0:T(8,128)(2,1)}, u32[]{:S(2)}) copy-start(bf16[3,64,64]{2,1,0:T(8,128)(2,1)} %param.29) | copy-start | bytes 73732
  0.7 28.4 %collective-permute-start = (bf16[2,6,4,4,1,1,128]{6,3,2,1,0,5,4:T(4,128)(2,1)S(1)}, bf16[2,6,4,4,1,1,128]{6,3,2,1,0,5,4:T(4,128)(2,1)S(1)}, u32[]{:S(2)}, u32[]{:S(2)}) collective-permute-start(bf16[2,6,4,4,1,1,128]{6,3,2,1,0,5,4:T(4,128)(2,1)S(1)} %get-tuple-element.197), channel_id=1, source_target_pairs={{0,16},{1,17},{2,18},{3,19},{4,20},{5,21},{6,22},{7,23},{8,24},{9,... | collective-permute-start | bytes 147464 | tf_op jit(solution)/shard_map/ppermute | solution.py:20
  5.8 23.3 %collective-permute-start.1 = (bf16[2,6,4,4,1,1,128]{6,3,2,1,0,5,4:T(4,128)(2,1)S(1)}, bf16[2,6,4,4,1,1,128]{6,3,2,1,0,5,4:T(4,128)(2,1)S(1)}, u32[]{:S(2)}, u32[]{:S(2)}) collective-permute-start(bf16[2,6,4,4,1,1,128]{6,3,2,1,0,5,4:T(4,128)(2,1)S(1)} %get-tuple-element.198), channel_id=1, source_target_pairs={{16,0},{17,1},{18,2},{19,3},{20,4},{21,5},{22,6},{23,7},{24,8},{25... | collective-permute-start | bytes 147464 | tf_op jit(solution)/shard_map/ppermute | solution.py:21
  7.1 22.0 %collective-permute-start.2 = (bf16[2,6,4,4,1,1,128]{6,3,2,1,0,5,4:T(4,128)(2,1)S(1)}, bf16[2,6,4,4,1,1,128]{6,3,2,1,0,5,4:T(4,128)(2,1)S(1)}, u32[]{:S(2)}, u32[]{:S(2)}) collective-permute-start(bf16[2,6,4,4,1,1,128]{6,3,2,1,0,5,4:T(4,128)(2,1)S(1)} %get-tuple-element.195), channel_id=1, source_target_pairs={{0,4},{4,8},{8,12},{1,5},{5,9},{9,13},{2,6},{6,10},{10,14},{3,7},{... | collective-permute-start | bytes 147464 | tf_op jit(solution)/shard_map/ppermute | solution.py:20
  8.6 20.5 %collective-permute-start.3 = (bf16[2,6,4,4,1,1,128]{6,3,2,1,0,5,4:T(4,128)(2,1)S(1)}, bf16[2,6,4,4,1,1,128]{6,3,2,1,0,5,4:T(4,128)(2,1)S(1)}, u32[]{:S(2)}, u32[]{:S(2)}) collective-permute-start(bf16[2,6,4,4,1,1,128]{6,3,2,1,0,5,4:T(4,128)(2,1)S(1)} %get-tuple-element.196), channel_id=1, source_target_pairs={{4,0},{8,4},{12,8},{5,1},{9,5},{13,9},{6,2},{10,6},{14,10},{7,3},{... | collective-permute-start | bytes 147464 | tf_op jit(solution)/shard_map/ppermute | solution.py:21
  11.7 10.5 %all-to-all-start = ((bf16[4,4,384]{2,1,0:T(4,128)(2,1)}), bf16[4,4,384]{2,1,0:T(4,128)(2,1)S(1)}, u32[]{:S(2)}, u32[]{:S(2)}) async-start(bf16[4,4,384]{2,1,0:T(4,128)(2,1)} %copy.260), calls=%async_computation | async-start | bytes 24576 | tf_op jit(solution)/shard_map/all_to_all | solution.py:155
  16.6 0.8 copy-start.9
  17.5 0.7 copy-start.17
  17.5 1.4 copy-start.18
  17.5 1.4 copy-start.13
  17.6 1.6 copy-start.19
  18.2 1.1 copy-start.12
  18.9 8.6 %copy-start.16 = (s32[128]{0:T(128)}, s32[128]{0:T(128)S(1)}, u32[]{:S(2)}) copy-start(s32[128]{0:T(128)S(1)} %fusion.77) | copy-start | bytes 1540
  19.2 8.0 %copy-start.14 = (f32[128]{0:T(128)}, f32[128]{0:T(128)S(1)}, u32[]{:S(2)}) copy-start(f32[128]{0:T(128)S(1)} %fusion.76) | copy-start | bytes 1540
  19.7 7.5 %copy-start.7 = (bf16[6,384]{1,0:T(8,128)(2,1)S(1)}, bf16[6,384]{1,0:T(8,128)(2,1)}, u32[]{:S(2)}) copy-start(bf16[6,384]{1,0:T(8,128)(2,1)} %param.32) | copy-start | bytes 13828
  22.2 6.8 %copy-start.3 = (bf16[1,6,64,1,1,128]{5,2,4,3,1,0:T(8,128)(2,1)S(1)}, bf16[1,6,64,1,1,128]{5,2,4,3,1,0:T(8,128)(2,1)}, u32[]{:S(2)}) copy-start(bf16[1,6,64,1,1,128]{5,2,4,3,1,0:T(8,128)(2,1)} %param.27) | copy-start | bytes 294916
  22.2 6.8 %copy-start.4 = (bf16[1,6,64,1,1,128]{5,2,4,3,1,0:T(8,128)(2,1)S(1)}, bf16[1,6,64,1,1,128]{5,2,4,3,1,0:T(8,128)(2,1)}, u32[]{:S(2)}) copy-start(bf16[1,6,64,1,1,128]{5,2,4,3,1,0:T(8,128)(2,1)} %param.26) | copy-start | bytes 294916
  29.0 0.7 copy-start.10
  31.5 10.2 %collective-permute-start.4 = (bf16[2,6,4,4,1,1,128]{6,3,2,1,0,5,4:T(4,128)(2,1)S(1)}, bf16[2,6,4,4,1,1,128]{6,3,2,1,0,5,4:T(4,128)(2,1)S(1)}, u32[]{:S(2)}, u32[]{:S(2)}) collective-permute-start(bf16[2,6,4,4,1,1,128]{6,3,2,1,0,5,4:T(4,128)(2,1)S(1)} %get-tuple-element.187), channel_id=1, source_target_pairs={{0,16},{1,17},{2,18},{3,19},{4,20},{5,21},{6,22},{7,23},{8,24},{9,... | collective-permute-start | bytes 147464 | tf_op jit(solution)/shard_map/ppermute | solution.py:20
  35.9 6.3 %collective-permute-start.5 = (bf16[2,6,4,4,1,1,128]{6,3,2,1,0,5,4:T(4,128)(2,1)S(1)}, bf16[2,6,4,4,1,1,128]{6,3,2,1,0,5,4:T(4,128)(2,1)S(1)}, u32[]{:S(2)}, u32[]{:S(2)}) collective-permute-start(bf16[2,6,4,4,1,1,128]{6,3,2,1,0,5,4:T(4,128)(2,1)S(1)} %get-tuple-element.188), channel_id=1, source_target_pairs={{16,0},{17,1},{18,2},{19,3},{20,4},{21,5},{22,6},{23,7},{24,8},{25... | collective-permute-start | bytes 147464 | tf_op jit(solution)/shard_map/ppermute | solution.py:21
  37.2 5.0 %collective-permute-start.6 = (bf16[2,6,4,4,1,1,128]{6,3,2,1,0,5,4:T(4,128)(2,1)S(1)}, bf16[2,6,4,4,1,1,128]{6,3,2,1,0,5,4:T(4,128)(2,1)S(1)}, u32[]{:S(2)}, u32[]{:S(2)}) collective-permute-start(bf16[2,6,4,4,1,1,128]{6,3,2,1,0,5,4:T(4,128)(2,1)S(1)} %get-tuple-element.185), channel_id=1, source_target_pairs={{0,4},{4,8},{8,12},{1,5},{5,9},{9,13},{2,6},{6,10},{10,14},{3,7},{... | collective-permute-start | bytes 147464 | tf_op jit(solution)/shard_map/ppermute | solution.py:20
  40.3 6.1 %collective-permute-start.7 = (bf16[2,6,4,4,1,1,128]{6,3,2,1,0,5,4:T(4,128)(2,1)S(1)}, bf16[2,6,4,4,1,1,128]{6,3,2,1,0,5,4:T(4,128)(2,1)S(1)}, u32[]{:S(2)}, u32[]{:S(2)}) collective-permute-start(bf16[2,6,4,4,1,1,128]{6,3,2,1,0,5,4:T(4,128)(2,1)S(1)} %get-tuple-element.186), channel_id=1, source_target_pairs={{4,0},{8,4},{12,8},{5,1},{9,5},{13,9},{6,2},{10,6},{14,10},{7,3},{... | collective-permute-start | bytes 147464 | tf_op jit(solution)/shard_map/ppermute | solution.py:21
  48.7 12.0 %collective-permute-start.10 = (bf16[2,6,4,4,1,1,128]{6,3,2,1,0,5,4:T(4,128)(2,1)S(1)}, bf16[2,6,4,4,1,1,128]{6,3,2,1,0,5,4:T(4,128)(2,1)S(1)}, u32[]{:S(2)}, u32[]{:S(2)}) collective-permute-start(bf16[2,6,4,4,1,1,128]{6,3,2,1,0,5,4:T(4,128)(2,1)S(1)} %get-tuple-element.175), channel_id=1, source_target_pairs={{0,4},{4,8},{8,12},{1,5},{5,9},{9,13},{2,6},{6,10},{10,14},{3,7},{... | collective-permute-start | bytes 147464 | tf_op jit(solution)/shard_map/ppermute | solution.py:20
  53.4 7.3 %collective-permute-start.11 = (bf16[2,6,4,4,1,1,128]{6,3,2,1,0,5,4:T(4,128)(2,1)S(1)}, bf16[2,6,4,4,1,1,128]{6,3,2,1,0,5,4:T(4,128)(2,1)S(1)}, u32[]{:S(2)}, u32[]{:S(2)}) collective-permute-start(bf16[2,6,4,4,1,1,128]{6,3,2,1,0,5,4:T(4,128)(2,1)S(1)} %get-tuple-element.176), channel_id=1, source_target_pairs={{4,0},{8,4},{12,8},{5,1},{9,5},{13,9},{6,2},{10,6},{14,10},{7,3},{... | collective-permute-start | bytes 147464 | tf_op jit(solution)/shard_map/ppermute | solution.py:21
  54.7 6.5 %collective-permute-start.8 = (bf16[2,6,4,4,1,1,128]{6,3,2,1,0,5,4:T(4,128)(2,1)S(1)}, bf16[2,6,4,4,1,1,128]{6,3,2,1,0,5,4:T(4,128)(2,1)S(1)}, u32[]{:S(2)}, u32[]{:S(2)}) collective-permute-start(bf16[2,6,4,4,1,1,128]{6,3,2,1,0,5,4:T(4,128)(2,1)S(1)} %get-tuple-element.177), channel_id=1, source_target_pairs={{0,16},{1,17},{2,18},{3,19},{4,20},{5,21},{6,22},{7,23},{8,24},{9,... | collective-permute-start | bytes 147464 | tf_op jit(solution)/shard_map/ppermute | solution.py:20
  59.3 6.4 %collective-permute-start.9 = (bf16[2,6,4,4,1,1,128]{6,3,2,1,0,5,4:T(4,128)(2,1)S(1)}, bf16[2,6,4,4,1,1,128]{6,3,2,1,0,5,4:T(4,128)(2,1)S(1)}, u32[]{:S(2)}, u32[]{:S(2)}) collective-permute-start(bf16[2,6,4,4,1,1,128]{6,3,2,1,0,5,4:T(4,128)(2,1)S(1)} %get-tuple-element.178), channel_id=1, source_target_pairs={{16,0},{17,1},{18,2},{19,3},{20,4},{21,5},{22,6},{23,7},{24,8},{25... | collective-permute-start | bytes 147464 | tf_op jit(solution)/shard_map/ppermute | solution.py:21
  71.2 51.5 %collective-permute-start.12 = (bf16[2,6,4,4,1,1,128]{6,3,2,1,0,5,4:T(4,128)(2,1)}, bf16[2,6,4,4,1,1,128]{6,3,2,1,0,5,4:T(4,128)(2,1)}, u32[]{:S(2)}, u32[]{:S(2)}) collective-permute-start(bf16[2,6,4,4,1,1,128]{6,3,2,1,0,5,4:T(4,128)(2,1)} %get-tuple-element.167), channel_id=1, source_target_pairs={{0,16},{1,17},{2,18},{3,19},{4,20},{5,21},{6,22},{7,23},{8,24},{9,... | collective-permute-start | bytes 147464 | tf_op jit(solution)/shard_map/ppermute | solution.py:20
  73.3 34.7 %copy-start.2 = (f32[6,64,128]{2,1,0:T(8,128)S(1)}, f32[6,64,128]{2,1,0:T(8,128)}, u32[]{:S(2)}) copy-start(f32[6,64,128]{2,1,0:T(8,128)} %multiply_reduce_fusion.12) | copy-start | bytes 589828
  103.2 10.7 %all-to-all-start.1 = ((f32[1,16,384]{2,0,1:T(1,128)}), f32[1,16,384]{2,0,1:T(1,128)}, u32[]{:S(2)}, u32[]{:S(2)}) async-start(f32[1,16,384]{2,0,1:T(1,128)} %psum.14), calls=%async_computation.1 | async-start | bytes 49152 | tf_op jit(solution)/shard_map/all_to_all | solution.py:184
  110.0 12.7 %collective-permute-start.13 = (bf16[2,6,4,4,1,1,128]{6,3,2,1,0,5,4:T(4,128)(2,1)}, bf16[2,6,4,4,1,1,128]{6,3,2,1,0,5,4:T(4,128)(2,1)S(1)}, u32[]{:S(2)}, u32[]{:S(2)}) collective-permute-start(bf16[2,6,4,4,1,1,128]{6,3,2,1,0,5,4:T(4,128)(2,1)} %get-tuple-element.168), channel_id=1, source_target_pairs={{16,0},{17,1},{18,2},{19,3},{20,4},{21,5},{22,6},{23,7},{24,8},{25... | collective-permute-start | bytes 147464 | tf_op jit(solution)/shard_map/ppermute | solution.py:21
  111.3 11.4 %collective-permute-start.14 = (bf16[2,6,4,4,1,1,128]{6,3,2,1,0,5,4:T(4,128)(2,1)}, bf16[2,6,4,4,1,1,128]{6,3,2,1,0,5,4:T(4,128)(2,1)S(1)}, u32[]{:S(2)}, u32[]{:S(2)}) collective-permute-start(bf16[2,6,4,4,1,1,128]{6,3,2,1,0,5,4:T(4,128)(2,1)} %get-tuple-element.165), channel_id=1, source_target_pairs={{0,4},{4,8},{8,12},{1,5},{5,9},{9,13},{2,6},{6,10},{10,14},{3,7},{... | collective-permute-start | bytes 147464 | tf_op jit(solution)/shard_map/ppermute | solution.py:20
  112.6 10.1 %collective-permute-start.15 = (bf16[2,6,4,4,1,1,128]{6,3,2,1,0,5,4:T(4,128)(2,1)}, bf16[2,6,4,4,1,1,128]{6,3,2,1,0,5,4:T(4,128)(2,1)S(1)}, u32[]{:S(2)}, u32[]{:S(2)}) collective-permute-start(bf16[2,6,4,4,1,1,128]{6,3,2,1,0,5,4:T(4,128)(2,1)} %get-tuple-element.166), channel_id=1, source_target_pairs={{4,0},{8,4},{12,8},{5,1},{9,5},{13,9},{6,2},{10,6},{14,10},{7,3},{... | collective-permute-start | bytes 147464 | tf_op jit(solution)/shard_map/ppermute | solution.py:21
  117.6 10.7 %all-to-all-start.2 = ((bf16[4,4,384]{2,1,0:T(4,128)(2,1)}), bf16[4,4,384]{2,1,0:T(4,128)(2,1)S(1)}, u32[]{:S(2)}, u32[]{:S(2)}) async-start(bf16[4,4,384]{2,1,0:T(4,128)(2,1)} %copy.301), calls=%async_computation.2 | async-start | bytes 24576 | tf_op jit(solution)/shard_map/all_to_all | solution.py:155
  123.9 9.4 %copy-start.15 = (f32[128]{0:T(128)S(1)}, f32[128]{0:T(128)}, u32[]{:S(2)}) copy-start(f32[128]{0:T(128)} %copy-done.14) | copy-start | bytes 1540
  128.3 6.9 %copy-start.5 = (bf16[1,6,64,1,1,128]{5,2,4,3,1,0:T(8,128)(2,1)S(1)}, bf16[1,6,64,1,1,128]{5,2,4,3,1,0:T(8,128)(2,1)}, u32[]{:S(2)}) copy-start(bf16[1,6,64,1,1,128]{5,2,4,3,1,0:T(8,128)(2,1)} %param.26) | copy-start | bytes 294916
  128.3 7.0 %copy-start.11 = (f32[6]{0:T(128)S(1)}, f32[6]{0:T(128)}, u32[]{:S(2)}) copy-start(f32[6]{0:T(128)} %param.30) | copy-start | bytes 76
  137.1 8.6 %collective-permute-start.16 = (bf16[2,6,4,4,1,1,128]{6,3,2,1,0,5,4:T(4,128)(2,1)S(1)}, bf16[2,6,4,4,1,1,128]{6,3,2,1,0,5,4:T(4,128)(2,1)S(1)}, u32[]{:S(2)}, u32[]{:S(2)}) collective-permute-start(bf16[2,6,4,4,1,1,128]{6,3,2,1,0,5,4:T(4,128)(2,1)S(1)} %get-tuple-element.157), channel_id=1, source_target_pairs={{0,16},{1,17},{2,18},{3,19},{4,20},{5,21},{6,22},{7,23},{8,24},{9,... | collective-permute-start | bytes 147464 | tf_op jit(solution)/shard_map/ppermute | solution.py:20
  141.7 6.0 %collective-permute-start.17 = (bf16[2,6,4,4,1,1,128]{6,3,2,1,0,5,4:T(4,128)(2,1)S(1)}, bf16[2,6,4,4,1,1,128]{6,3,2,1,0,5,4:T(4,128)(2,1)S(1)}, u32[]{:S(2)}, u32[]{:S(2)}) collective-permute-start(bf16[2,6,4,4,1,1,128]{6,3,2,1,0,5,4:T(4,128)(2,1)S(1)} %get-tuple-element.158), channel_id=1, source_target_pairs={{16,0},{17,1},{18,2},{19,3},{20,4},{21,5},{22,6},{23,7},{24,8},{25... | collective-permute-start | bytes 147464 | tf_op jit(solution)/shard_map/ppermute | solution.py:21
  143.0 4.7 %collective-permute-start.18 = (bf16[2,6,4,4,1,1,128]{6,3,2,1,0,5,4:T(4,128)(2,1)S(1)}, bf16[2,6,4,4,1,1,128]{6,3,2,1,0,5,4:T(4,128)(2,1)S(1)}, u32[]{:S(2)}, u32[]{:S(2)}) collective-permute-start(bf16[2,6,4,4,1,1,128]{6,3,2,1,0,5,4:T(4,128)(2,1)S(1)} %get-tuple-element.155), channel_id=1, source_target_pairs={{0,4},{4,8},{8,12},{1,5},{5,9},{9,13},{2,6},{6,10},{10,14},{3,7},{... | collective-permute-start | bytes 147464 | tf_op jit(solution)/shard_map/ppermute | solution.py:20
  144.3 5.3 %collective-permute-start.19 = (bf16[2,6,4,4,1,1,128]{6,3,2,1,0,5,4:T(4,128)(2,1)S(1)}, bf16[2,6,4,4,1,1,128]{6,3,2,1,0,5,4:T(4,128)(2,1)S(1)}, u32[]{:S(2)}, u32[]{:S(2)}) collective-permute-start(bf16[2,6,4,4,1,1,128]{6,3,2,1,0,5,4:T(4,128)(2,1)S(1)} %get-tuple-element.156), channel_id=1, source_target_pairs={{4,0},{8,4},{12,8},{5,1},{9,5},{13,9},{6,2},{10,6},{14,10},{7,3},{... | collective-permute-start | bytes 147464 | tf_op jit(solution)/shard_map/ppermute | solution.py:21
  151.2 12.3 %collective-permute-start.20 = (bf16[2,6,4,4,1,1,128]{6,3,2,1,0,5,4:T(4,128)(2,1)S(1)}, bf16[2,6,4,4,1,1,128]{6,3,2,1,0,5,4:T(4,128)(2,1)S(1)}, u32[]{:S(2)}, u32[]{:S(2)}) collective-permute-start(bf16[2,6,4,4,1,1,128]{6,3,2,1,0,5,4:T(4,128)(2,1)S(1)} %get-tuple-element.147), channel_id=1, source_target_pairs={{0,16},{1,17},{2,18},{3,19},{4,20},{5,21},{6,22},{7,23},{8,24},{9,... | collective-permute-start | bytes 147464 | tf_op jit(solution)/shard_map/ppermute | solution.py:20
  155.7 7.8 %collective-permute-start.21 = (bf16[2,6,4,4,1,1,128]{6,3,2,1,0,5,4:T(4,128)(2,1)S(1)}, bf16[2,6,4,4,1,1,128]{6,3,2,1,0,5,4:T(4,128)(2,1)S(1)}, u32[]{:S(2)}, u32[]{:S(2)}) collective-permute-start(bf16[2,6,4,4,1,1,128]{6,3,2,1,0,5,4:T(4,128)(2,1)S(1)} %get-tuple-element.148), channel_id=1, source_target_pairs={{16,0},{17,1},{18,2},{19,3},{20,4},{21,5},{22,6},{23,7},{24,8},{25... | collective-permute-start | bytes 147464 | tf_op jit(solution)/shard_map/ppermute | solution.py:21
  157.0 6.5 %collective-permute-start.22 = (bf16[2,6,4,4,1,1,128]{6,3,2,1,0,5,4:T(4,128)(2,1)S(1)}, bf16[2,6,4,4,1,1,128]{6,3,2,1,0,5,4:T(4,128)(2,1)S(1)}, u32[]{:S(2)}, u32[]{:S(2)}) collective-permute-start(bf16[2,6,4,4,1,1,128]{6,3,2,1,0,5,4:T(4,128)(2,1)S(1)} %get-tuple-element.145), channel_id=1, source_target_pairs={{0,4},{4,8},{8,12},{1,5},{5,9},{9,13},{2,6},{6,10},{10,14},{3,7},{... | collective-permute-start | bytes 147464 | tf_op jit(solution)/shard_map/ppermute | solution.py:20
  161.4 3.1 %collective-permute-start.23 = (bf16[2,6,4,4,1,1,128]{6,3,2,1,0,5,4:T(4,128)(2,1)S(1)}, bf16[2,6,4,4,1,1,128]{6,3,2,1,0,5,4:T(4,128)(2,1)S(1)}, u32[]{:S(2)}, u32[]{:S(2)}) collective-permute-start(bf16[2,6,4,4,1,1,128]{6,3,2,1,0,5,4:T(4,128)(2,1)S(1)} %get-tuple-element.146), channel_id=1, source_target_pairs={{4,0},{8,4},{12,8},{5,1},{9,5},{13,9},{6,2},{10,6},{14,10},{7,3},{... | collective-permute-start | bytes 147464 | tf_op jit(solution)/shard_map/ppermute | solution.py:21
  165.1 40.2 %copy-start.8 = (f32[4,4,384]{2,1,0:T(4,128)S(1)}, f32[4,4,384]{2,1,0:T(4,128)}, u32[]{:S(2)}) copy-start(f32[4,4,384]{2,1,0:T(4,128)} %param.35) | copy-start | bytes 73732
  166.0 39.8 %copy-start.6 = (f32[4,4,384]{2,1,0:T(4,128)S(1)}, f32[4,4,384]{2,1,0:T(4,128)}, u32[]{:S(2)}) copy-start(f32[4,4,384]{2,1,0:T(4,128)} %param.34) | copy-start | bytes 73732
where the time goes:
time: 209 us; the launch traced here: 208 us
  starting transfers between devices  70.7 us (34%)
  blocking collectives  56.4 us (27%)
  other arithmetic  28.5 us (14%)
  local copies, waits for them, and re-layouts  21.8 us (10%)
  waiting for transfers between devices  20 us (10%)
  matrix products  7.17 us (3%)
  between operations  2.87 us (1%)
    psum x2, blocking collectives, body(): summed = lax.psum(partial_loads, ('fx', 'fy'))  48.4 us
    ppermute x12, starting transfers between devices, with_halo(): before = lax.ppermute(last, axis, up)  41.3 us
    ppermute x12, starting transfers between devices, with_halo(): after = lax.ppermute(initial, axis, down)  15.5 us
    ppermute x12, waiting for transfers between devices, with_halo(): after = lax.ppermute(initial, axis, down)  13.9 us
    gather x2, local copies, waits for them, and re-layouts, body(): picked = received.reshape(-1)[columns]  10 us
    all_to_all x2, starting transfers between devices, body(): lax.all_to_all(shell_tangent.astype(jnp.bfloat16), 'st', split_axis=0, co...  9.96 us
    scatter-add x2, other arithmetic, body(): jnp.zeros((panels * SDOF * PN,), jnp.float32).at[columns].add(loads)  9.5 us
    all_to_all x1, blocking collectives, body(): lax.all_to_all(summed, 'st', split_axis=1, concat_axis=0, tiled=True)  7.97 us
  transfers between devices with their start and end apart: 27, of which 9 were waited for; matrix products, arithmetic and copies ran while one was open for 13% of the time, Pallas kernels for 0%

commit v1 on v0

--- a/solution.py
+++ b/solution.py
@@ -180,7 +180,7 @@
         panels = received.shape[1]
         partial_loads = jnp.zeros((panels * SDOF * PN,), jnp.float32).at[columns].add(loads)
         partial_loads = partial_loads.reshape(1, panels, SDOF * PN)
-        summed = lax.psum(partial_loads, ("fx", "fy"))
+        summed = lax.psum(lax.psum(partial_loads, "fx"), "fy")
         owned = lax.all_to_all(summed, "st", split_axis=1, concat_axis=0, tiled=True)
         shell_adjoint = shell_solve(shell_adjoint_rhs - owned)
         shell_tangent = shell_solve(shell_load + shell_adjoint)

time: 209 us -> 202 us (0.967)
  blocking collectives: 56.4 us -> 46.2 us
  starting transfers between devices: 70.7 us -> 72.9 us
    psum x2 -> x4, blocking collectives: 48.4 us -> 38.2 us  [body(): summed = lax.psum(lax.psum(partial_loads, 'fx'), 'fy')]
    ppermute x12, starting transfers between devices: 41.3 us -> 43.9 us  [with_halo(): before = lax.ppermute(last, axis, up)]
  transfers between devices with their start and end apart: 27 -> 27, of which waited for: 9 -> 9; matrix products, arithmetic and copies ran while one was open for 13% -> 14% of each run, Pallas kernels for 0% -> 0%
where the time goes in v1:
time: 202 us; the launch traced here: 200 us
  starting transfers between devices  72.9 us (36%)
  blocking collectives  46.2 us (23%)
  other arithmetic  28.5 us (14%)
  local copies, waits for them, and re-layouts  21.8 us (11%)
  waiting for transfers between devices  20.8 us (10%)
  matrix products  7.17 us (4%)
  between operations  2.87 us (1%)
    ppermute x12, starting transfers between devices, with_halo(): before = lax.ppermute(last, axis, up)  43.9 us
    psum x4, blocking collectives, body(): summed = lax.psum(lax.psum(partial_loads, 'fx'), 'fy')  38.2 us
    ppermute x12, starting transfers between devices, with_halo(): after = lax.ppermute(initial, axis, down)  15.5 us
    ppermute x12, waiting for transfers between devices, with_halo(): after = lax.ppermute(initial, axis, down)  14.7 us
    gather x2, local copies, waits for them, and re-layouts, body(): picked = received.reshape(-1)[columns]  10 us
    all_to_all x2, starting transfers between devices, body(): lax.all_to_all(shell_tangent.astype(jnp.bfloat16), 'st', split_axis=0, co...  9.63 us
    scatter-add x2, other arithmetic, body(): jnp.zeros((panels * SDOF * PN,), jnp.float32).at[columns].add(loads)  9.5 us
    all_to_all x1, blocking collectives, body(): lax.all_to_all(summed, 'st', split_axis=1, concat_axis=0, tiled=True)  7.97 us
  transfers between devices with their start and end apart: 27, of which 9 were waited for; matrix products, arithmetic and copies ran while one was open for 14% of the time, Pallas kernels for 0%

profile of v1, /device:TPU:0, one launch (start us, length us, event | category | flops | bytes accessed | tf_op | source)
XLA Modules:
  0.0 200.3 jit_solution(4026703729437026718)
XLA Ops:
  0.7 5.0 %collective-permute-start = (bf16[2,6,4,4,1,1,128]{6,3,2,1,0,5,4:T(4,128)(2,1)S(1)}, bf16[2,6,4,4,1,1,128]{6,3,2,1,0,5,4:T(4,128)(2,1)S(1)}, u32[]{:S(2)}, u32[]{:S(2)}) collective-permute-start(bf16[2,6,4,4,1,1,128]{6,3,2,1,0,5,4:T(4,128)(2,1)S(1)} %get-tuple-element.197), channel_id=1, source_target_pairs={{0,16},{1,17},{2,18},{3,19},{4,20},{5,21},{6,22},{7,23},{8,24},{9,... | collective-permute-start | bytes 147464 | tf_op jit(solution)/shard_map/ppermute | solution.py:20
  5.8 1.3 collective-permute-start.1
  7.1 1.5 collective-permute-start.2
  8.6 1.3 collective-permute-start.3
  9.9 0.7 convert_element_type.279
  11.1 0.6 copy.260
  11.7 4.9 %all-to-all-start = ((bf16[4,4,384]{2,1,0:T(4,128)(2,1)}), bf16[4,4,384]{2,1,0:T(4,128)(2,1)S(1)}, u32[]{:S(2)}, u32[]{:S(2)}) async-start(bf16[4,4,384]{2,1,0:T(4,128)(2,1)} %copy.260), calls=%async_computation | async-start | bytes 24576 | tf_op jit(solution)/shard_map/all_to_all | solution.py:155
  21.0 1.2 all-to-all-done
  22.2 5.0 %gather_fusion = bf16[768]{0:T(1024)(128)(2,1)S(1)} fusion(bf16[6144]{0:T(1024)(128)(2,1)S(1)} %reshape.2599, s32[1024]{0:T(1024)S(1)} %pad_clamp_fusion.1), kind=kCustom, calls=%fused_computation | custom fusion | bytes 6144 | tf_op jit(solution)/shard_map/gather | solution.py:158
  27.5 1.4 scatter_custom_fusion
  31.5 4.4 %collective-permute-start.4 = (bf16[2,6,4,4,1,1,128]{6,3,2,1,0,5,4:T(4,128)(2,1)S(1)}, bf16[2,6,4,4,1,1,128]{6,3,2,1,0,5,4:T(4,128)(2,1)S(1)}, u32[]{:S(2)}, u32[]{:S(2)}) collective-permute-start(bf16[2,6,4,4,1,1,128]{6,3,2,1,0,5,4:T(4,128)(2,1)S(1)} %get-tuple-element.187), channel_id=1, source_target_pairs={{0,16},{1,17},{2,18},{3,19},{4,20},{5,21},{6,22},{7,23},{8,24},{9,... | collective-permute-start | bytes 147464 | tf_op jit(solution)/shard_map/ppermute | solution.py:20
  35.9 1.3 collective-permute-start.5
  37.2 3.0 %collective-permute-start.6 = (bf16[2,6,4,4,1,1,128]{6,3,2,1,0,5,4:T(4,128)(2,1)S(1)}, bf16[2,6,4,4,1,1,128]{6,3,2,1,0,5,4:T(4,128)(2,1)S(1)}, u32[]{:S(2)}, u32[]{:S(2)}) collective-permute-start(bf16[2,6,4,4,1,1,128]{6,3,2,1,0,5,4:T(4,128)(2,1)S(1)} %get-tuple-element.185), channel_id=1, source_target_pairs={{0,4},{4,8},{8,12},{1,5},{5,9},{9,13},{2,6},{6,10},{10,14},{3,7},{... | collective-permute-start | bytes 147464 | tf_op jit(solution)/shard_map/ppermute | solution.py:20
  40.3 1.3 collective-permute-start.7
  42.3 4.1 %collective-permute-done.7 = bf16[2,6,4,4,1,1,128]{6,3,2,1,0,5,4:T(4,128)(2,1)S(1)} collective-permute-done((bf16[2,6,4,4,1,1,128]{6,3,2,1,0,5,4:T(4,128)(2,1)S(1)}, bf16[2,6,4,4,1,1,128]{6,3,2,1,0,5,4:T(4,128)(2,1)S(1)}, u32[]{:S(2)}, u32[]{:S(2)}) %collective-permute-start.7) | collective-permute-done | bytes 49184 | tf_op jit(solution)/shard_map/ppermute | solution.py:21
  48.7 4.7 %collective-permute-start.10 = (bf16[2,6,4,4,1,1,128]{6,3,2,1,0,5,4:T(4,128)(2,1)S(1)}, bf16[2,6,4,4,1,1,128]{6,3,2,1,0,5,4:T(4,128)(2,1)S(1)}, u32[]{:S(2)}, u32[]{:S(2)}) collective-permute-start(bf16[2,6,4,4,1,1,128]{6,3,2,1,0,5,4:T(4,128)(2,1)S(1)} %get-tuple-element.175), channel_id=1, source_target_pairs={{0,4},{4,8},{8,12},{1,5},{5,9},{9,13},{2,6},{6,10},{10,14},{3,7},{... | collective-permute-start | bytes 147464 | tf_op jit(solution)/shard_map/ppermute | solution.py:20
  53.4 1.3 collective-permute-start.11
  54.7 4.5 %collective-permute-start.8 = (bf16[2,6,4,4,1,1,128]{6,3,2,1,0,5,4:T(4,128)(2,1)S(1)}, bf16[2,6,4,4,1,1,128]{6,3,2,1,0,5,4:T(4,128)(2,1)S(1)}, u32[]{:S(2)}, u32[]{:S(2)}) collective-permute-start(bf16[2,6,4,4,1,1,128]{6,3,2,1,0,5,4:T(4,128)(2,1)S(1)} %get-tuple-element.177), channel_id=1, source_target_pairs={{0,16},{1,17},{2,18},{3,19},{4,20},{5,21},{6,22},{7,23},{8,24},{9,... | collective-permute-start | bytes 147464 | tf_op jit(solution)/shard_map/ppermute | solution.py:20
  59.3 1.3 collective-permute-start.9
  61.2 4.4 %collective-permute-done.9 = bf16[2,6,4,4,1,1,128]{6,3,2,1,0,5,4:T(4,128)(2,1)S(1)} collective-permute-done((bf16[2,6,4,4,1,1,128]{6,3,2,1,0,5,4:T(4,128)(2,1)S(1)}, bf16[2,6,4,4,1,1,128]{6,3,2,1,0,5,4:T(4,128)(2,1)S(1)}, u32[]{:S(2)}, u32[]{:S(2)}) %collective-permute-start.9) | collective-permute-done | bytes 49184 | tf_op jit(solution)/shard_map/ppermute | solution.py:21
  66.9 0.7 slice_bitcast_fusion.71
  67.6 0.7 slice_bitcast_fusion.69
  68.6 0.8 multiply_reduce_fusion.12
  69.5 0.8 multiply_reduce_fusion.14
  70.4 0.8 slice.579
  71.2 2.1 %collective-permute-start.12 = (bf16[2,6,4,4,1,1,128]{6,3,2,1,0,5,4:T(4,128)(2,1)}, bf16[2,6,4,4,1,1,128]{6,3,2,1,0,5,4:T(4,128)(2,1)}, u32[]{:S(2)}, u32[]{:S(2)}) collective-permute-start(bf16[2,6,4,4,1,1,128]{6,3,2,1,0,5,4:T(4,128)(2,1)} %get-tuple-element.167), channel_id=1, source_target_pairs={{0,16},{1,17},{2,18},{3,19},{4,20},{5,21},{6,22},{7,23},{8,24},{9,... | collective-permute-start | bytes 147464 | tf_op jit(solution)/shard_map/ppermute | solution.py:20
  73.4 1.1 gather_fusion.1
  74.5 0.8 fusion.5
  75.3 4.8 %scatter_custom_fusion.1 = f32[6144]{0:T(1024)S(1)} fusion(s32[768]{0:T(1024)} %copy-done.12, f32[768]{0:T(1024)S(1)} %fusion.5, f32[]{:T(128)} %constant.129.clone.1), kind=kCustom, calls=%fused_computation.296 | custom fusion | flops 768 | bytes 25088 | tf_op jit(solution)/shard_map/scatter-add | solution.py:181
  80.0 7.0 %psum.28 = f32[1,16,384]{2,0,1:T(1,128)S(1)} all-reduce(f32[1,16,384]{2,0,1:T(1,128)S(1)} %bitcast.739), channel_id=1, replica_groups=mesh['fx'=2,'fy'=4,'st'=4] {'fx'}, use_global_device_ids=true, to_apply=%region_20.27 | all-reduce | flops 6144 | bytes 49152 | tf_op jit(solution)/shard_map/psum | solution.py:183
  87.0 10.8 %psum.29 = f32[1,16,384]{2,0,1:T(1,128)} all-reduce(f32[1,16,384]{2,0,1:T(1,128)S(1)} %psum.28), channel_id=1, replica_groups=mesh['fx'=2,'fy'=4,'st'=4] {'fy'}, use_global_device_ids=true, to_apply=%region_21.28 | all-reduce | flops 6144 | bytes 49152 | tf_op jit(solution)/shard_map/psum | solution.py:183
  97.9 3.9 %all-to-all-start.1 = ((f32[1,16,384]{2,0,1:T(1,128)}), f32[1,16,384]{2,0,1:T(1,128)}, u32[]{:S(2)}, u32[]{:S(2)}) async-start(f32[1,16,384]{2,0,1:T(1,128)} %psum.29), calls=%async_computation.1 | async-start | bytes 49152 | tf_op jit(solution)/shard_map/all_to_all | solution.py:184
  101.8 0.9 convert_add_fusion
  102.8 1.0 add_bitcast_fusion.4
  103.7 0.9 pad_subtract_fusion.4
  104.7 1.3 collective-permute-start.13
  106.0 2.3 %collective-permute-start.14 = (bf16[2,6,4,4,1,1,128]{6,3,2,1,0,5,4:T(4,128)(2,1)}, bf16[2,6,4,4,1,1,128]{6,3,2,1,0,5,4:T(4,128)(2,1)S(1)}, u32[]{:S(2)}, u32[]{:S(2)}) collective-permute-start(bf16[2,6,4,4,1,1,128]{6,3,2,1,0,5,4:T(4,128)(2,1)} %get-tuple-element.165), channel_id=1, source_target_pairs={{0,4},{4,8},{8,12},{1,5},{5,9},{9,13},{2,6},{6,10},{10,14},{3,7},{... | collective-permute-start | bytes 147464 | tf_op jit(solution)/shard_map/ppermute | solution.py:20
  108.3 1.3 collective-permute-start.15
  109.6 0.8 reduce.36
  110.4 0.7 subtract_convert_fusion.1
  111.1 1.5 fusion.3
  112.6 0.6 copy.301
  113.3 4.8 %all-to-all-start.2 = ((bf16[4,4,384]{2,1,0:T(4,128)(2,1)}), bf16[4,4,384]{2,1,0:T(4,128)(2,1)S(1)}, u32[]{:S(2)}, u32[]{:S(2)}) async-start(bf16[4,4,384]{2,1,0:T(4,128)(2,1)} %copy.301), calls=%async_computation.2 | async-start | bytes 24576 | tf_op jit(solution)/shard_map/all_to_all | solution.py:155
  118.1 0.9 subtract_bitcast_fusion.9
  119.3 4.4 %all-to-all-done.2 = bf16[4,4,384]{2,1,0:T(4,128)(2,1)S(1)} async-done(((bf16[4,4,384]{2,1,0:T(4,128)(2,1)}), bf16[4,4,384]{2,1,0:T(4,128)(2,1)S(1)}, u32[]{:S(2)}, u32[]{:S(2)}) %all-to-all-start.2) | async-done | bytes 12320 | tf_op jit(solution)/shard_map/all_to_all | solution.py:155
  123.7 5.0 %gather_fusion.2 = bf16[768]{0:T(1024)(128)(2,1)S(1)} fusion(bf16[6144]{0:T(1024)(128)(2,1)S(1)} %reshape.2612, s32[1024]{0:T(1024)S(1)} %pad_clamp_fusion.1), kind=kCustom, calls=%fused_computation.2 | custom fusion | bytes 6144 | tf_op jit(solution)/shard_map/gather | solution.py:158
  128.9 1.5 scatter_custom_fusion.2
  132.5 4.3 %collective-permute-start.16 = (bf16[2,6,4,4,1,1,128]{6,3,2,1,0,5,4:T(4,128)(2,1)S(1)}, bf16[2,6,4,4,1,1,128]{6,3,2,1,0,5,4:T(4,128)(2,1)S(1)}, u32[]{:S(2)}, u32[]{:S(2)}) collective-permute-start(bf16[2,6,4,4,1,1,128]{6,3,2,1,0,5,4:T(4,128)(2,1)S(1)} %get-tuple-element.157), channel_id=1, source_target_pairs={{0,16},{1,17},{2,18},{3,19},{4,20},{5,21},{6,22},{7,23},{8,24},{9,... | collective-permute-start | bytes 147464 | tf_op jit(solution)/shard_map/ppermute | solution.py:20
  136.8 1.3 collective-permute-start.17
  138.1 3.2 %collective-permute-start.18 = (bf16[2,6,4,4,1,1,128]{6,3,2,1,0,5,4:T(4,128)(2,1)S(1)}, bf16[2,6,4,4,1,1,128]{6,3,2,1,0,5,4:T(4,128)(2,1)S(1)}, u32[]{:S(2)}, u32[]{:S(2)}) collective-permute-start(bf16[2,6,4,4,1,1,128]{6,3,2,1,0,5,4:T(4,128)(2,1)S(1)} %get-tuple-element.155), channel_id=1, source_target_pairs={{0,4},{4,8},{8,12},{1,5},{5,9},{9,13},{2,6},{6,10},{10,14},{3,7},{... | collective-permute-start | bytes 147464 | tf_op jit(solution)/shard_map/ppermute | solution.py:20
  141.2 1.3 collective-permute-start.19
  143.0 4.3 %collective-permute-done.19 = bf16[2,6,4,4,1,1,128]{6,3,2,1,0,5,4:T(4,128)(2,1)S(1)} collective-permute-done((bf16[2,6,4,4,1,1,128]{6,3,2,1,0,5,4:T(4,128)(2,1)S(1)}, bf16[2,6,4,4,1,1,128]{6,3,2,1,0,5,4:T(4,128)(2,1)S(1)}, u32[]{:S(2)}, u32[]{:S(2)}) %collective-permute-start.19) | collective-permute-done | bytes 49184 | tf_op jit(solution)/shard_map/ppermute | solution.py:21
  148.9 4.5 %collective-permute-start.20 = (bf16[2,6,4,4,1,1,128]{6,3,2,1,0,5,4:T(4,128)(2,1)S(1)}, bf16[2,6,4,4,1,1,128]{6,3,2,1,0,5,4:T(4,128)(2,1)S(1)}, u32[]{:S(2)}, u32[]{:S(2)}) collective-permute-start(bf16[2,6,4,4,1,1,128]{6,3,2,1,0,5,4:T(4,128)(2,1)S(1)} %get-tuple-element.147), channel_id=1, source_target_pairs={{0,16},{1,17},{2,18},{3,19},{4,20},{5,21},{6,22},{7,23},{8,24},{9,... | collective-permute-start | bytes 147464 | tf_op jit(solution)/shard_map/ppermute | solution.py:20
  153.5 1.3 collective-permute-start.21
  154.8 4.4 %collective-permute-start.22 = (bf16[2,6,4,4,1,1,128]{6,3,2,1,0,5,4:T(4,128)(2,1)S(1)}, bf16[2,6,4,4,1,1,128]{6,3,2,1,0,5,4:T(4,128)(2,1)S(1)}, u32[]{:S(2)}, u32[]{:S(2)}) collective-permute-start(bf16[2,6,4,4,1,1,128]{6,3,2,1,0,5,4:T(4,128)(2,1)S(1)} %get-tuple-element.145), channel_id=1, source_target_pairs={{0,4},{4,8},{8,12},{1,5},{5,9},{9,13},{2,6},{6,10},{10,14},{3,7},{... | collective-permute-start | bytes 147464 | tf_op jit(solution)/shard_map/ppermute | solution.py:20
  159.2 1.3 collective-permute-start.23
  161.3 1.0 collective-permute-done.23
  162.9 0.7 fusion.87
  163.8 1.1 gather_fusion.3
  165.0 4.8 %scatter_custom_fusion.3 = f32[6144]{0:T(1024)S(1)} fusion(s32[768]{0:T(1024)} %copy-done.12, f32[768]{0:T(1024)S(1)} %fusion.4, f32[]{:T(128)} %constant.129.clone.1), kind=kCustom, calls=%fused_computation.294 | custom fusion | flops 768 | bytes 25088 | tf_op jit(solution)/shard_map/scatter-add | solution.py:181
  169.8 9.2 %psum.30 = f32[1,16,384]{2,0,1:T(1,128)S(1)} all-reduce(f32[1,16,384]{2,0,1:T(1,128)S(1)} %bitcast.738), channel_id=1, replica_groups=mesh['fx'=2,'fy'=4,'st'=4] {'fx'}, use_global_device_ids=true, to_apply=%region_42.49 | all-reduce | flops 6144 | bytes 49152 | tf_op jit(solution)/shard_map/psum | solution.py:183
  179.0 11.1 %psum.31 = f32[1,16,384]{2,0,1:T(1,128)S(1)} all-reduce(f32[1,16,384]{2,0,1:T(1,128)S(1)} %psum.30), channel_id=1, replica_groups=mesh['fx'=2,'fy'=4,'st'=4] {'fy'}, use_global_device_ids=true, to_apply=%region_43.50 | all-reduce | flops 6144 | bytes 49152 | tf_op jit(solution)/shard_map/psum | solution.py:183
  190.1 8.0 %all_to_all.42 = f32[1,16,384]{2,0,1:T(1,128)S(1)} all-to-all(f32[1,16,384]{2,0,1:T(1,128)S(1)} %psum.31), channel_id=1, replica_groups=mesh['fx'=2,'fy'=4,'st'=4] {'st'}, dimensions={1} | all-to-all | bytes 49152 | tf_op jit(solution)/shard_map/all_to_all | solution.py:184
  199.1 0.6 copy.339
  (226 shorter events, 19.8 us)
Async XLA Ops:
  0.6 10.0 %copy-start = (bf16[4,384,384]{2,1,0:T(8,128)(2,1)S(1)}, bf16[4,384,384]{2,1,0:T(8,128)(2,1)}, u32[]{:S(2)}) copy-start(bf16[4,384,384]{2,1,0:T(8,128)(2,1)} %param.33) | copy-start | bytes 3538948
  0.6 16.1 %copy-start.1 = (bf16[3,64,64]{2,1,0:T(8,128)(2,1)S(1)}, bf16[3,64,64]{2,1,0:T(8,128)(2,1)}, u32[]{:S(2)}) copy-start(bf16[3,64,64]{2,1,0:T(8,128)(2,1)} %param.29) | copy-start | bytes 73732
  0.7 28.4 %collective-permute-start = (bf16[2,6,4,4,1,1,128]{6,3,2,1,0,5,4:T(4,128)(2,1)S(1)}, bf16[2,6,4,4,1,1,128]{6,3,2,1,0,5,4:T(4,128)(2,1)S(1)}, u32[]{:S(2)}, u32[]{:S(2)}) collective-permute-start(bf16[2,6,4,4,1,1,128]{6,3,2,1,0,5,4:T(4,128)(2,1)S(1)} %get-tuple-element.197), channel_id=1, source_target_pairs={{0,16},{1,17},{2,18},{3,19},{4,20},{5,21},{6,22},{7,23},{8,24},{9,... | collective-permute-start | bytes 147464 | tf_op jit(solution)/shard_map/ppermute | solution.py:20
  5.8 23.3 %collective-permute-start.1 = (bf16[2,6,4,4,1,1,128]{6,3,2,1,0,5,4:T(4,128)(2,1)S(1)}, bf16[2,6,4,4,1,1,128]{6,3,2,1,0,5,4:T(4,128)(2,1)S(1)}, u32[]{:S(2)}, u32[]{:S(2)}) collective-permute-start(bf16[2,6,4,4,1,1,128]{6,3,2,1,0,5,4:T(4,128)(2,1)S(1)} %get-tuple-element.198), channel_id=1, source_target_pairs={{16,0},{17,1},{18,2},{19,3},{20,4},{21,5},{22,6},{23,7},{24,8},{25... | collective-permute-start | bytes 147464 | tf_op jit(solution)/shard_map/ppermute | solution.py:21
  7.1 22.0 %collective-permute-start.2 = (bf16[2,6,4,4,1,1,128]{6,3,2,1,0,5,4:T(4,128)(2,1)S(1)}, bf16[2,6,4,4,1,1,128]{6,3,2,1,0,5,4:T(4,128)(2,1)S(1)}, u32[]{:S(2)}, u32[]{:S(2)}) collective-permute-start(bf16[2,6,4,4,1,1,128]{6,3,2,1,0,5,4:T(4,128)(2,1)S(1)} %get-tuple-element.195), channel_id=1, source_target_pairs={{0,4},{4,8},{8,12},{1,5},{5,9},{9,13},{2,6},{6,10},{10,14},{3,7},{... | collective-permute-start | bytes 147464 | tf_op jit(solution)/shard_map/ppermute | solution.py:20
  8.6 20.5 %collective-permute-start.3 = (bf16[2,6,4,4,1,1,128]{6,3,2,1,0,5,4:T(4,128)(2,1)S(1)}, bf16[2,6,4,4,1,1,128]{6,3,2,1,0,5,4:T(4,128)(2,1)S(1)}, u32[]{:S(2)}, u32[]{:S(2)}) collective-permute-start(bf16[2,6,4,4,1,1,128]{6,3,2,1,0,5,4:T(4,128)(2,1)S(1)} %get-tuple-element.196), channel_id=1, source_target_pairs={{4,0},{8,4},{12,8},{5,1},{9,5},{13,9},{6,2},{10,6},{14,10},{7,3},{... | collective-permute-start | bytes 147464 | tf_op jit(solution)/shard_map/ppermute | solution.py:21
  11.7 10.5 %all-to-all-start = ((bf16[4,4,384]{2,1,0:T(4,128)(2,1)}), bf16[4,4,384]{2,1,0:T(4,128)(2,1)S(1)}, u32[]{:S(2)}, u32[]{:S(2)}) async-start(bf16[4,4,384]{2,1,0:T(4,128)(2,1)} %copy.260), calls=%async_computation | async-start | bytes 24576 | tf_op jit(solution)/shard_map/all_to_all | solution.py:155
  16.6 0.8 copy-start.9
  17.5 0.7 copy-start.17
  17.5 1.4 copy-start.18
  17.5 1.4 copy-start.13
  17.6 1.6 copy-start.19
  18.2 1.1 copy-start.12
  18.9 8.6 %copy-start.16 = (s32[128]{0:T(128)}, s32[128]{0:T(128)S(1)}, u32[]{:S(2)}) copy-start(s32[128]{0:T(128)S(1)} %fusion.77) | copy-start | bytes 1540
  19.2 8.0 %copy-start.14 = (f32[128]{0:T(128)}, f32[128]{0:T(128)S(1)}, u32[]{:S(2)}) copy-start(f32[128]{0:T(128)S(1)} %fusion.76) | copy-start | bytes 1540
  19.7 7.5 %copy-start.7 = (bf16[6,384]{1,0:T(8,128)(2,1)S(1)}, bf16[6,384]{1,0:T(8,128)(2,1)}, u32[]{:S(2)}) copy-start(bf16[6,384]{1,0:T(8,128)(2,1)} %param.32) | copy-start | bytes 13828
  22.2 6.8 %copy-start.3 = (bf16[1,6,64,1,1,128]{5,2,4,3,1,0:T(8,128)(2,1)S(1)}, bf16[1,6,64,1,1,128]{5,2,4,3,1,0:T(8,128)(2,1)}, u32[]{:S(2)}) copy-start(bf16[1,6,64,1,1,128]{5,2,4,3,1,0:T(8,128)(2,1)} %param.27) | copy-start | bytes 294916
  22.2 6.8 %copy-start.4 = (bf16[1,6,64,1,1,128]{5,2,4,3,1,0:T(8,128)(2,1)S(1)}, bf16[1,6,64,1,1,128]{5,2,4,3,1,0:T(8,128)(2,1)}, u32[]{:S(2)}) copy-start(bf16[1,6,64,1,1,128]{5,2,4,3,1,0:T(8,128)(2,1)} %param.26) | copy-start | bytes 294916
  29.0 0.7 copy-start.10
  31.5 10.2 %collective-permute-start.4 = (bf16[2,6,4,4,1,1,128]{6,3,2,1,0,5,4:T(4,128)(2,1)S(1)}, bf16[2,6,4,4,1,1,128]{6,3,2,1,0,5,4:T(4,128)(2,1)S(1)}, u32[]{:S(2)}, u32[]{:S(2)}) collective-permute-start(bf16[2,6,4,4,1,1,128]{6,3,2,1,0,5,4:T(4,128)(2,1)S(1)} %get-tuple-element.187), channel_id=1, source_target_pairs={{0,16},{1,17},{2,18},{3,19},{4,20},{5,21},{6,22},{7,23},{8,24},{9,... | collective-permute-start | bytes 147464 | tf_op jit(solution)/shard_map/ppermute | solution.py:20
  35.9 6.3 %collective-permute-start.5 = (bf16[2,6,4,4,1,1,128]{6,3,2,1,0,5,4:T(4,128)(2,1)S(1)}, bf16[2,6,4,4,1,1,128]{6,3,2,1,0,5,4:T(4,128)(2,1)S(1)}, u32[]{:S(2)}, u32[]{:S(2)}) collective-permute-start(bf16[2,6,4,4,1,1,128]{6,3,2,1,0,5,4:T(4,128)(2,1)S(1)} %get-tuple-element.188), channel_id=1, source_target_pairs={{16,0},{17,1},{18,2},{19,3},{20,4},{21,5},{22,6},{23,7},{24,8},{25... | collective-permute-start | bytes 147464 | tf_op jit(solution)/shard_map/ppermute | solution.py:21
  37.2 5.0 %collective-permute-start.6 = (bf16[2,6,4,4,1,1,128]{6,3,2,1,0,5,4:T(4,128)(2,1)S(1)}, bf16[2,6,4,4,1,1,128]{6,3,2,1,0,5,4:T(4,128)(2,1)S(1)}, u32[]{:S(2)}, u32[]{:S(2)}) collective-permute-start(bf16[2,6,4,4,1,1,128]{6,3,2,1,0,5,4:T(4,128)(2,1)S(1)} %get-tuple-element.185), channel_id=1, source_target_pairs={{0,4},{4,8},{8,12},{1,5},{5,9},{9,13},{2,6},{6,10},{10,14},{3,7},{... | collective-permute-start | bytes 147464 | tf_op jit(solution)/shard_map/ppermute | solution.py:20
  40.3 6.1 %collective-permute-start.7 = (bf16[2,6,4,4,1,1,128]{6,3,2,1,0,5,4:T(4,128)(2,1)S(1)}, bf16[2,6,4,4,1,1,128]{6,3,2,1,0,5,4:T(4,128)(2,1)S(1)}, u32[]{:S(2)}, u32[]{:S(2)}) collective-permute-start(bf16[2,6,4,4,1,1,128]{6,3,2,1,0,5,4:T(4,128)(2,1)S(1)} %get-tuple-element.186), channel_id=1, source_target_pairs={{4,0},{8,4},{12,8},{5,1},{9,5},{13,9},{6,2},{10,6},{14,10},{7,3},{... | collective-permute-start | bytes 147464 | tf_op jit(solution)/shard_map/ppermute | solution.py:21
  48.7 12.0 %collective-permute-start.10 = (bf16[2,6,4,4,1,1,128]{6,3,2,1,0,5,4:T(4,128)(2,1)S(1)}, bf16[2,6,4,4,1,1,128]{6,3,2,1,0,5,4:T(4,128)(2,1)S(1)}, u32[]{:S(2)}, u32[]{:S(2)}) collective-permute-start(bf16[2,6,4,4,1,1,128]{6,3,2,1,0,5,4:T(4,128)(2,1)S(1)} %get-tuple-element.175), channel_id=1, source_target_pairs={{0,4},{4,8},{8,12},{1,5},{5,9},{9,13},{2,6},{6,10},{10,14},{3,7},{... | collective-permute-start | bytes 147464 | tf_op jit(solution)/shard_map/ppermute | solution.py:20
  53.4 7.3 %collective-permute-start.11 = (bf16[2,6,4,4,1,1,128]{6,3,2,1,0,5,4:T(4,128)(2,1)S(1)}, bf16[2,6,4,4,1,1,128]{6,3,2,1,0,5,4:T(4,128)(2,1)S(1)}, u32[]{:S(2)}, u32[]{:S(2)}) collective-permute-start(bf16[2,6,4,4,1,1,128]{6,3,2,1,0,5,4:T(4,128)(2,1)S(1)} %get-tuple-element.176), channel_id=1, source_target_pairs={{4,0},{8,4},{12,8},{5,1},{9,5},{13,9},{6,2},{10,6},{14,10},{7,3},{... | collective-permute-start | bytes 147464 | tf_op jit(solution)/shard_map/ppermute | solution.py:21
  54.7 6.5 %collective-permute-start.8 = (bf16[2,6,4,4,1,1,128]{6,3,2,1,0,5,4:T(4,128)(2,1)S(1)}, bf16[2,6,4,4,1,1,128]{6,3,2,1,0,5,4:T(4,128)(2,1)S(1)}, u32[]{:S(2)}, u32[]{:S(2)}) collective-permute-start(bf16[2,6,4,4,1,1,128]{6,3,2,1,0,5,4:T(4,128)(2,1)S(1)} %get-tuple-element.177), channel_id=1, source_target_pairs={{0,16},{1,17},{2,18},{3,19},{4,20},{5,21},{6,22},{7,23},{8,24},{9,... | collective-permute-start | bytes 147464 | tf_op jit(solution)/shard_map/ppermute | solution.py:20
  59.3 6.4 %collective-permute-start.9 = (bf16[2,6,4,4,1,1,128]{6,3,2,1,0,5,4:T(4,128)(2,1)S(1)}, bf16[2,6,4,4,1,1,128]{6,3,2,1,0,5,4:T(4,128)(2,1)S(1)}, u32[]{:S(2)}, u32[]{:S(2)}) collective-permute-start(bf16[2,6,4,4,1,1,128]{6,3,2,1,0,5,4:T(4,128)(2,1)S(1)} %get-tuple-element.178), channel_id=1, source_target_pairs={{16,0},{17,1},{18,2},{19,3},{20,4},{21,5},{22,6},{23,7},{24,8},{25... | collective-permute-start | bytes 147464 | tf_op jit(solution)/shard_map/ppermute | solution.py:21
  71.2 46.9 %collective-permute-start.12 = (bf16[2,6,4,4,1,1,128]{6,3,2,1,0,5,4:T(4,128)(2,1)}, bf16[2,6,4,4,1,1,128]{6,3,2,1,0,5,4:T(4,128)(2,1)}, u32[]{:S(2)}, u32[]{:S(2)}) collective-permute-start(bf16[2,6,4,4,1,1,128]{6,3,2,1,0,5,4:T(4,128)(2,1)} %get-tuple-element.167), channel_id=1, source_target_pairs={{0,16},{1,17},{2,18},{3,19},{4,20},{5,21},{6,22},{7,23},{8,24},{9,... | collective-permute-start | bytes 147464 | tf_op jit(solution)/shard_map/ppermute | solution.py:20
  73.3 29.4 %copy-start.2 = (f32[6,64,128]{2,1,0:T(8,128)S(1)}, f32[6,64,128]{2,1,0:T(8,128)}, u32[]{:S(2)}) copy-start(f32[6,64,128]{2,1,0:T(8,128)} %multiply_reduce_fusion.12) | copy-start | bytes 589828
  97.9 11.7 %all-to-all-start.1 = ((f32[1,16,384]{2,0,1:T(1,128)}), f32[1,16,384]{2,0,1:T(1,128)}, u32[]{:S(2)}, u32[]{:S(2)}) async-start(f32[1,16,384]{2,0,1:T(1,128)} %psum.29), calls=%async_computation.1 | async-start | bytes 49152 | tf_op jit(solution)/shard_map/all_to_all | solution.py:184
  104.7 13.4 %collective-permute-start.13 = (bf16[2,6,4,4,1,1,128]{6,3,2,1,0,5,4:T(4,128)(2,1)}, bf16[2,6,4,4,1,1,128]{6,3,2,1,0,5,4:T(4,128)(2,1)S(1)}, u32[]{:S(2)}, u32[]{:S(2)}) collective-permute-start(bf16[2,6,4,4,1,1,128]{6,3,2,1,0,5,4:T(4,128)(2,1)} %get-tuple-element.168), channel_id=1, source_target_pairs={{16,0},{17,1},{18,2},{19,3},{20,4},{21,5},{22,6},{23,7},{24,8},{25... | collective-permute-start | bytes 147464 | tf_op jit(solution)/shard_map/ppermute | solution.py:21
  106.0 12.1 %collective-permute-start.14 = (bf16[2,6,4,4,1,1,128]{6,3,2,1,0,5,4:T(4,128)(2,1)}, bf16[2,6,4,4,1,1,128]{6,3,2,1,0,5,4:T(4,128)(2,1)S(1)}, u32[]{:S(2)}, u32[]{:S(2)}) collective-permute-start(bf16[2,6,4,4,1,1,128]{6,3,2,1,0,5,4:T(4,128)(2,1)} %get-tuple-element.165), channel_id=1, source_target_pairs={{0,4},{4,8},{8,12},{1,5},{5,9},{9,13},{2,6},{6,10},{10,14},{3,7},{... | collective-permute-start | bytes 147464 | tf_op jit(solution)/shard_map/ppermute | solution.py:20
  108.3 9.8 %collective-permute-start.15 = (bf16[2,6,4,4,1,1,128]{6,3,2,1,0,5,4:T(4,128)(2,1)}, bf16[2,6,4,4,1,1,128]{6,3,2,1,0,5,4:T(4,128)(2,1)S(1)}, u32[]{:S(2)}, u32[]{:S(2)}) collective-permute-start(bf16[2,6,4,4,1,1,128]{6,3,2,1,0,5,4:T(4,128)(2,1)} %get-tuple-element.166), channel_id=1, source_target_pairs={{4,0},{8,4},{12,8},{5,1},{9,5},{13,9},{6,2},{10,6},{14,10},{7,3},{... | collective-permute-start | bytes 147464 | tf_op jit(solution)/shard_map/ppermute | solution.py:21
  113.3 10.4 %all-to-all-start.2 = ((bf16[4,4,384]{2,1,0:T(4,128)(2,1)}), bf16[4,4,384]{2,1,0:T(4,128)(2,1)S(1)}, u32[]{:S(2)}, u32[]{:S(2)}) async-start(bf16[4,4,384]{2,1,0:T(4,128)(2,1)} %copy.301), calls=%async_computation.2 | async-start | bytes 24576 | tf_op jit(solution)/shard_map/all_to_all | solution.py:155
  119.3 9.4 %copy-start.15 = (f32[128]{0:T(128)S(1)}, f32[128]{0:T(128)}, u32[]{:S(2)}) copy-start(f32[128]{0:T(128)} %copy-done.14) | copy-start | bytes 1540
  123.7 6.9 %copy-start.5 = (bf16[1,6,64,1,1,128]{5,2,4,3,1,0:T(8,128)(2,1)S(1)}, bf16[1,6,64,1,1,128]{5,2,4,3,1,0:T(8,128)(2,1)}, u32[]{:S(2)}) copy-start(bf16[1,6,64,1,1,128]{5,2,4,3,1,0:T(8,128)(2,1)} %param.26) | copy-start | bytes 294916
  123.7 7.0 %copy-start.11 = (f32[6]{0:T(128)S(1)}, f32[6]{0:T(128)}, u32[]{:S(2)}) copy-start(f32[6]{0:T(128)} %param.30) | copy-start | bytes 76
  132.5 10.2 %collective-permute-start.16 = (bf16[2,6,4,4,1,1,128]{6,3,2,1,0,5,4:T(4,128)(2,1)S(1)}, bf16[2,6,4,4,1,1,128]{6,3,2,1,0,5,4:T(4,128)(2,1)S(1)}, u32[]{:S(2)}, u32[]{:S(2)}) collective-permute-start(bf16[2,6,4,4,1,1,128]{6,3,2,1,0,5,4:T(4,128)(2,1)S(1)} %get-tuple-element.157), channel_id=1, source_target_pairs={{0,16},{1,17},{2,18},{3,19},{4,20},{5,21},{6,22},{7,23},{8,24},{9,... | collective-permute-start | bytes 147464 | tf_op jit(solution)/shard_map/ppermute | solution.py:20
  136.8 6.2 %collective-permute-start.17 = (bf16[2,6,4,4,1,1,128]{6,3,2,1,0,5,4:T(4,128)(2,1)S(1)}, bf16[2,6,4,4,1,1,128]{6,3,2,1,0,5,4:T(4,128)(2,1)S(1)}, u32[]{:S(2)}, u32[]{:S(2)}) collective-permute-start(bf16[2,6,4,4,1,1,128]{6,3,2,1,0,5,4:T(4,128)(2,1)S(1)} %get-tuple-element.158), channel_id=1, source_target_pairs={{16,0},{17,1},{18,2},{19,3},{20,4},{21,5},{22,6},{23,7},{24,8},{25... | collective-permute-start | bytes 147464 | tf_op jit(solution)/shard_map/ppermute | solution.py:21
  138.1 4.9 %collective-permute-start.18 = (bf16[2,6,4,4,1,1,128]{6,3,2,1,0,5,4:T(4,128)(2,1)S(1)}, bf16[2,6,4,4,1,1,128]{6,3,2,1,0,5,4:T(4,128)(2,1)S(1)}, u32[]{:S(2)}, u32[]{:S(2)}) collective-permute-start(bf16[2,6,4,4,1,1,128]{6,3,2,1,0,5,4:T(4,128)(2,1)S(1)} %get-tuple-element.155), channel_id=1, source_target_pairs={{0,4},{4,8},{8,12},{1,5},{5,9},{9,13},{2,6},{6,10},{10,14},{3,7},{... | collective-permute-start | bytes 147464 | tf_op jit(solution)/shard_map/ppermute | solution.py:20
  141.2 6.1 %collective-permute-start.19 = (bf16[2,6,4,4,1,1,128]{6,3,2,1,0,5,4:T(4,128)(2,1)S(1)}, bf16[2,6,4,4,1,1,128]{6,3,2,1,0,5,4:T(4,128)(2,1)S(1)}, u32[]{:S(2)}, u32[]{:S(2)}) collective-permute-start(bf16[2,6,4,4,1,1,128]{6,3,2,1,0,5,4:T(4,128)(2,1)S(1)} %get-tuple-element.156), channel_id=1, source_target_pairs={{4,0},{8,4},{12,8},{5,1},{9,5},{13,9},{6,2},{10,6},{14,10},{7,3},{... | collective-permute-start | bytes 147464 | tf_op jit(solution)/shard_map/ppermute | solution.py:21
  148.9 12.3 %collective-permute-start.20 = (bf16[2,6,4,4,1,1,128]{6,3,2,1,0,5,4:T(4,128)(2,1)S(1)}, bf16[2,6,4,4,1,1,128]{6,3,2,1,0,5,4:T(4,128)(2,1)S(1)}, u32[]{:S(2)}, u32[]{:S(2)}) collective-permute-start(bf16[2,6,4,4,1,1,128]{6,3,2,1,0,5,4:T(4,128)(2,1)S(1)} %get-tuple-element.147), channel_id=1, source_target_pairs={{0,16},{1,17},{2,18},{3,19},{4,20},{5,21},{6,22},{7,23},{8,24},{9,... | collective-permute-start | bytes 147464 | tf_op jit(solution)/shard_map/ppermute | solution.py:20
  153.5 7.8 %collective-permute-start.21 = (bf16[2,6,4,4,1,1,128]{6,3,2,1,0,5,4:T(4,128)(2,1)S(1)}, bf16[2,6,4,4,1,1,128]{6,3,2,1,0,5,4:T(4,128)(2,1)S(1)}, u32[]{:S(2)}, u32[]{:S(2)}) collective-permute-start(bf16[2,6,4,4,1,1,128]{6,3,2,1,0,5,4:T(4,128)(2,1)S(1)} %get-tuple-element.148), channel_id=1, source_target_pairs={{16,0},{17,1},{18,2},{19,3},{20,4},{21,5},{22,6},{23,7},{24,8},{25... | collective-permute-start | bytes 147464 | tf_op jit(solution)/shard_map/ppermute | solution.py:21
  154.8 6.5 %collective-permute-start.22 = (bf16[2,6,4,4,1,1,128]{6,3,2,1,0,5,4:T(4,128)(2,1)S(1)}, bf16[2,6,4,4,1,1,128]{6,3,2,1,0,5,4:T(4,128)(2,1)S(1)}, u32[]{:S(2)}, u32[]{:S(2)}) collective-permute-start(bf16[2,6,4,4,1,1,128]{6,3,2,1,0,5,4:T(4,128)(2,1)S(1)} %get-tuple-element.145), channel_id=1, source_target_pairs={{0,4},{4,8},{8,12},{1,5},{5,9},{9,13},{2,6},{6,10},{10,14},{3,7},{... | collective-permute-start | bytes 147464 | tf_op jit(solution)/shard_map/ppermute | solution.py:20
  159.2 3.1 %collective-permute-start.23 = (bf16[2,6,4,4,1,1,128]{6,3,2,1,0,5,4:T(4,128)(2,1)S(1)}, bf16[2,6,4,4,1,1,128]{6,3,2,1,0,5,4:T(4,128)(2,1)S(1)}, u32[]{:S(2)}, u32[]{:S(2)}) collective-permute-start(bf16[2,6,4,4,1,1,128]{6,3,2,1,0,5,4:T(4,128)(2,1)S(1)} %get-tuple-element.146), channel_id=1, source_target_pairs={{4,0},{8,4},{12,8},{5,1},{9,5},{13,9},{6,2},{10,6},{14,10},{7,3},{... | collective-permute-start | bytes 147464 | tf_op jit(solution)/shard_map/ppermute | solution.py:21
  162.9 35.3 %copy-start.8 = (f32[4,4,384]{2,1,0:T(4,128)S(1)}, f32[4,4,384]{2,1,0:T(4,128)}, u32[]{:S(2)}) copy-start(f32[4,4,384]{2,1,0:T(4,128)} %param.35) | copy-start | bytes 73732
  163.8 34.9 %copy-start.6 = (f32[4,4,384]{2,1,0:T(4,128)S(1)}, f32[4,4,384]{2,1,0:T(4,128)}, u32[]{:S(2)}) copy-start(f32[4,4,384]{2,1,0:T(4,128)} %param.34) | copy-start | bytes 73732
